TPU v7x, 32 devices: a whole 2x2x4 slice. The times are simulated.
32 devices in a mesh: group: 2 (over x), lon: 8 (over z, y), lat: 2 (over core).
Axes of the slice: x: 2, y: 2, z: 4, core: 2. Of those that a mesh axis runs over, the one named last changes fastest.
Arguments:
- tokens: bfloat16 [128, 256, 384], P(('group', 'lat'), 'lon'), parts along dimension 0, may hold values from -6 to 6
- visible: int32 [128, 256], P(('group', 'lat'), 'lon'), parts along dimension 0, may hold values 0 or 1
- mask_token: bfloat16 [384], replicated, may hold values from -4 to 4
- norm_gain_table: float32 [2, 384], replicated, may hold values from 0.25 to 1.75
- query_key_value_weight: bfloat16 [2, 384, 1152], replicated, may hold values from -0.3125 to 0.3125
- output_weight: bfloat16 [2, 384, 384], replicated, may hold values from -0.3125 to 0.3125
- cotangent: float32 [128, 256, 384], P(('group', 'lat'), 'lon'), parts along dimension 0, may hold values from -6 to 6
Outputs:
- grad_tokens: float32 [128, 256, 384], P(('group', 'lat'), 'lon'), parts along dimension 0
- grad_qkv: float32 [4, 384, 1152], P('group'), parts along dimension 0
- grad_out: float32 [4, 384, 384], P('group'), parts along dimension 0
- grad_gain: float32 [4, 384], P('group'), parts along dimension 0
There are 2 independent parts, one for each index of `group`. A program takes and returns all parts, laid end to end along the dimension named above; an argument that names none is the same for every part. Nothing has to cross between parts.
Inputs may be any that keep to these rules, and one draw needn't show every extreme that they name: 1 marks a visible token.
All inputs are finite; a program needn't handle non-finite values. No bound on the sum of `visible` on one device may be relied on, other than what follows from the above.
Results may differ from a plain program's by a relative error of at most 0.01.
Values may be sent and summed in bfloat16 or wider, within the bound.
No kernel may reach another device: no remote copies, remote signals or barrier semaphores. Data moves between devices by JAX's collectives and lax.ppermute only.
A program may use at most 320 MiB of HBM per device.

v0:
```python
import jax
import jax.numpy as jnp
from jax import lax
from jax.sharding import PartitionSpec as P

HEADS = 6


def partner(value, axis, stride):
    mask = 2**stride
    pairs = [(source, source ^ mask) for source in range(lax.axis_size(axis))]
    return lax.ppermute(value, axis, pairs)


def passed_along(value, axis, steps):
    count = lax.axis_size(axis)
    pairs = [(source, (source + steps) % count) for source in range(count)]
    return lax.ppermute(value, axis, pairs)


def extended_2(cells, sides, width):
    for axis, dim in sides:
        count = lax.axis_size(axis)
        head = lax.slice_in_dim(cells, 0, width, axis=dim)
        tail = lax.slice_in_dim(cells, cells.shape[dim] - width, cells.shape[dim], axis=dim)
        cells = jnp.concatenate(
            [
                lax.ppermute(tail, axis, [(i, (i + 1) % count) for i in range(count)]),
                cells,
                lax.ppermute(head, axis, [((i + 1) % count, i) for i in range(count)]),
            ],
            axis=dim,
        )
    return cells


def normed(values_in, gain_row):
    mean_value = jnp.mean(values_in, axis=-1, keepdims=True)
    centred = values_in - mean_value
    spread = jnp.mean(centred * centred, axis=-1, keepdims=True)
    return centred * lax.rsqrt(spread + 1e-05) * gain_row


def mix_heads(query_heads, key_list, value_list, mask_list):
    head_size = query_heads.shape[1]
    weights = []
    for key_one, mask_one in zip(key_list, mask_list):
        weight_one = jnp.exp(jnp.sum(query_heads * key_one, axis=1) * head_size ** (-0.5))
        if mask_one is not None:
            weight_one = weight_one * mask_one
        weights.append(weight_one)
    weight_sum = sum(weights)
    result = jnp.zeros_like(query_heads)
    for weight_one, value_one in zip(weights, value_list):
        result = result + (weight_one / weight_sum)[:, None, :] * value_one
    return result


def dilated_mix(query_flat, blocks):
    width = query_flat.shape[0]
    head_size = width // HEADS
    points = query_flat.shape[1]
    query_heads = query_flat.reshape(HEADS, head_size, points)
    key_list = [
        blocks[number, :width].reshape(HEADS, head_size, points)
        for number in range(blocks.shape[0])
    ]
    value_list = [
        blocks[number, width:].reshape(HEADS, head_size, points)
        for number in range(blocks.shape[0])
    ]
    mask_list = [None for number in range(blocks.shape[0])]
    return mix_heads(query_heads, key_list, value_list, mask_list).reshape(width, points)


def plain_mix(query_grid, padded, lat_masks, grid_rows, grid_cols, margin):
    width = query_grid.shape[0]
    head_size = width // HEADS
    points = grid_rows * grid_cols
    placed = jnp.pad(query_grid, ((0, 0), (1, 1), (1, 1))).reshape(HEADS, head_size, points)
    key_list = []
    value_list = []
    mask_list = []
    for lat_step in (-1, 0, 1):
        for lon_step in (-1, 0, 1):
            start_at = margin + lat_step * grid_cols + lon_step
            window = padded[:, start_at : start_at + points]
            key_list.append(window[:width].reshape(HEADS, head_size, points))
            value_list.append(window[width:].reshape(HEADS, head_size, points))
            mask_list.append(lat_masks[lat_step + 1])
    result = mix_heads(placed, key_list, value_list, mask_list).reshape(width, grid_rows, grid_cols)
    return result[:, 1 : grid_rows - 1, 1 : grid_cols - 1]


def surround(block_in):
    partner_block = partner(block_in, "lat", 0)
    pair_blocks = jnp.stack([block_in, partner_block])
    moved_blocks = [passed_along(pair_blocks, "lon", step_dir) for step_dir in (1, -1)]
    return jnp.concatenate([pair_blocks, moved_blocks[0], moved_blocks[1]], 0)


def gather_back(grad_blocks):
    pair_blocks = grad_blocks[0:2]
    for step_dir, rim_part in ((-1, grad_blocks[2:4]), (1, grad_blocks[4:6])):
        pair_blocks = pair_blocks + passed_along(
            rim_part.astype(jnp.bfloat16), "lon", step_dir
        ).astype(rim_part.dtype)
    return pair_blocks[0] + partner(pair_blocks[1].astype(jnp.bfloat16), "lat", 0).astype(
        jnp.float32
    )


def widen_plain(keyval_grid):
    row_count = keyval_grid.shape[1]
    is_upper = lax.axis_index("lat") == 0
    outgoing = jnp.where(is_upper, keyval_grid[:, row_count - 1 :], keyval_grid[:, :1])
    partner_row = partner(outgoing, "lat", 0)
    empty_row = jnp.zeros_like(partner_row)
    lat_band = jnp.where(
        is_upper,
        jnp.concatenate([empty_row, keyval_grid, partner_row], 1),
        jnp.concatenate([partner_row, keyval_grid, empty_row], 1),
    )
    return extended_2(lat_band, (("lon", 2),), 1)


def fold_plain(grad_grid):
    grid_rows = grad_grid.shape[1]
    grid_cols = grad_grid.shape[2]
    col_count = grid_cols - 2
    row_count = grid_rows - 2
    core_part = grad_grid[:, :, 1 : grid_cols - 1]
    for step_dir, rim_part in ((-1, grad_grid[:, :, :1]), (1, grad_grid[:, :, grid_cols - 1 :])):
        arrived = passed_along(rim_part.astype(jnp.bfloat16), "lon", step_dir).astype(
            rim_part.dtype
        )
        before = col_count - 1 if step_dir == -1 else 0
        core_part = core_part + jnp.pad(arrived, ((0, 0), (0, 0), (before, col_count - 1 - before)))
    is_upper = lax.axis_index("lat") == 0
    outgoing = jnp.where(is_upper, core_part[:, grid_rows - 1 :], core_part[:, :1])
    returned = partner(outgoing.astype(jnp.bfloat16), "lat", 0).astype(outgoing.dtype)
    own_part = core_part[:, 1 : grid_rows - 1]
    placed = jnp.where(
        is_upper,
        jnp.pad(returned, ((0, 0), (row_count - 1, 0), (0, 0))),
        jnp.pad(returned, ((0, 0), (0, row_count - 1), (0, 0))),
    )
    return own_part + placed


def project_features(normal_flat, weight_part):
    return jnp.einsum(
        "nd,de->en", normal_flat, weight_part, preferred_element_type=jnp.float32
    ).astype(jnp.bfloat16)


def forward_layer(layer_in, gain_row, weight_qkv, weight_out, dilated):
    row_count, col_count, width = layer_in.shape
    points = row_count * col_count
    normal_part, norm_pull = jax.vjp(normed, layer_in, gain_row)
    normal_half = normal_part.astype(jnp.bfloat16).reshape(points, width)
    query_flat = project_features(normal_half, weight_qkv[:, :width])
    grid_info = None
    if dilated:
        wide_input = normal_half
        blocks = surround(project_features(normal_half, weight_qkv[:, width:]))
        mixed_flat, attend_pull = jax.vjp(
            dilated_mix, query_flat.astype(jnp.float32), blocks.astype(jnp.float32)
        )
    else:
        wide_input = normal_half
        keyval_grid = project_features(normal_half, weight_qkv[:, width:]).reshape(
            2 * width, row_count, col_count
        )
        extended = widen_plain(keyval_grid)
        grid_rows = row_count + 2
        grid_cols = col_count + 2
        margin = grid_cols + 1
        grid_points = grid_rows * grid_cols
        padded = jnp.pad(extended.reshape(2 * width, grid_points), ((0, 0), (margin, margin)))
        row_index = jnp.arange(grid_points, dtype=jnp.int32) // grid_cols
        outside_row = jnp.where(lax.axis_index("lat") == 0, 0, grid_rows - 1)
        lat_masks = []
        for lat_step in (-1, 0, 1):
            target = row_index + lat_step
            lat_masks.append(
                jnp.where(
                    (target >= 0) & (target <= grid_rows - 1) & (target != outside_row), 1.0, 0.0
                ).astype(jnp.float32)
            )

        def local_mix(query_grid, padded_in):
            return plain_mix(query_grid, padded_in, lat_masks, grid_rows, grid_cols, margin)

        query_grid = query_flat.astype(jnp.float32).reshape(width, row_count, col_count)
        mixed_grid, attend_pull = jax.vjp(local_mix, query_grid, padded.astype(jnp.float32))
        mixed_flat = mixed_grid.reshape(width, points)
        grid_info = (grid_rows, grid_cols, margin)
    mixed_half = mixed_flat.astype(jnp.bfloat16)
    layer_out = layer_in.reshape(points, width) + jnp.einsum(
        "dn,de->ne", mixed_half, weight_out, preferred_element_type=jnp.float32
    )
    saved = (
        norm_pull,
        attend_pull,
        normal_half,
        wide_input,
        mixed_half,
        dilated,
        grid_info,
        (row_count, col_count),
    )
    return (layer_out.reshape(row_count, col_count, width), saved)


def backward_layer(grad_in, saved, weight_qkv, weight_out):
    norm_pull, attend_pull, normal_half, wide_input, mixed_half, dilated, grid_info, shape_info = (
        saved
    )
    row_count, col_count = shape_info
    points, width = normal_half.shape
    highest = lax.Precision.HIGHEST
    weight_full = weight_qkv.astype(jnp.float32)
    normal_full = normal_half.astype(jnp.float32)
    grad_mixed = jnp.einsum("ne,de->dn", grad_in, weight_out.astype(jnp.float32), precision=highest)
    grad_wout = jnp.einsum("dn,ne->de", mixed_half.astype(jnp.float32), grad_in, precision=highest)
    if dilated:
        grad_query, grad_blocks = attend_pull(grad_mixed)
    else:
        grad_query_grid, grad_padded = attend_pull(grad_mixed.reshape(width, row_count, col_count))
        grad_query = grad_query_grid.reshape(width, points)
        grid_rows, grid_cols, margin = grid_info
        grad_grid = grad_padded[:, margin : margin + grid_rows * grid_cols].reshape(
            2 * width, grid_rows, grid_cols
        )
        grad_blocks = fold_plain(grad_grid).reshape(2 * width, points)
    grad_normal = jnp.einsum("en,de->nd", grad_query, weight_full[:, :width], precision=highest)
    grad_wquery = jnp.einsum("nd,en->de", normal_full, grad_query, precision=highest)
    grad_kvown = gather_back(grad_blocks) if dilated else grad_blocks
    grad_wkv = jnp.einsum("nd,en->de", normal_full, grad_kvown, precision=highest)
    grad_normal = grad_normal + jnp.einsum(
        "en,de->nd", grad_kvown, weight_full[:, width:], precision=highest
    )
    grad_field, grad_gain = norm_pull(grad_normal.reshape(row_count, col_count, width))
    return (
        grad_in + grad_field.reshape(points, width),
        jnp.concatenate([grad_wquery, grad_wkv], axis=1),
        grad_wout,
        grad_gain,
    )


def local(
    tokens, visible, mask_token, norm_gain_table, query_key_value_weight, output_weight, cotangent
):
    row_count, col_count, width = tokens.shape
    lat_count = lax.axis_size("lat")
    lon_count = lax.axis_size("lon")
    shown = visible[..., None] == 1
    starting_tokens = jnp.where(
        shown, tokens.astype(jnp.float32), mask_token.astype(jnp.float32)[None, None, :]
    )
    between_tokens, saved_first = forward_layer(
        starting_tokens, norm_gain_table[0], query_key_value_weight[0], output_weight[0], True
    )
    middle_half = lax.optimization_barrier(between_tokens.astype(jnp.bfloat16)).astype(jnp.float32)
    unused_final, saved_second = forward_layer(
        middle_half, norm_gain_table[1], query_key_value_weight[1], output_weight[1], False
    )
    grad_final = cotangent.reshape(row_count * col_count, width)
    gradient_between, qkv_second, out_second, gain_second = backward_layer(
        grad_final, saved_second, query_key_value_weight[1], output_weight[1]
    )
    grad_start, qkv_first, out_first, gain_first = backward_layer(
        gradient_between, saved_first, query_key_value_weight[0], output_weight[0]
    )
    grad_tokens = jnp.where(shown, grad_start.reshape(row_count, col_count, width), 0.0)
    summed_qkv, summed_out, summed_gain = lax.psum(
        (
            jnp.stack([qkv_first, qkv_second]),
            jnp.stack([out_first, out_second]),
            jnp.stack([gain_first, gain_second]),
        ),
        ("lon", "lat"),
    )
    factor = (row_count * col_count * lat_count * lon_count) ** (-0.5)
    return (grad_tokens, summed_qkv * factor, summed_out * factor, summed_gain * factor)


def solution(mesh):
    return jax.shard_map(
        local,
        mesh=mesh,
        in_specs=(
            P(("group", "lat"), "lon", None),
            P(("group", "lat"), "lon"),
            P(),
            P(),
            P(),
            P(),
            P(("group", "lat"), "lon", None),
        ),
        out_specs=(
            P(("group", "lat"), "lon", None),
            P("group", None, None),
            P("group", None, None),
            P("group", None),
        ),
        check_vma=False,
    )
```

profile of v0, /device:TPU:0, one launch (start us, length us, event | category | flops | bytes accessed | tf_op | source)
XLA Modules:
  0.0 959.3 jit_solution(4182502671617775337)
XLA Ops:
  43.2 119.3 %collective-permute-done.1 = bf16[2,768,1024]{2,1,0:T(8,128)(2,1)} collective-permute-done((bf16[2,768,1024]{2,1,0:T(8,128)(2,1)}, bf16[2,768,1024]{2,1,0:T(8,128)(2,1)}, u32[]{:S(2)}, u32[]{:S(2)}) %collective-permute-start.1) | collective-permute-done | bytes 3145760 | tf_op jit(solution)/shard_map/ppermute | solution.py:18
  165.2 4.8 maximum_convert_fusion
  170.0 6.6 fusion.90
  176.6 5.4 copy-done
  182.1 6.0 multiply_reduce_fusion.26
  195.5 4.9 collective-permute-start.5
  213.8 10.1 %fusion.92 = (f32[384,1156]{0,1:T(8,128)}, f32[384,1156]{0,1:T(8,128)}, f32[384,1156]{0,1:T(8,128)}, f32[384,1156]{0,1:T(8,128)}, f32[384,1156]{0,1:T(8,128)}, /...) fusion(f32[768,1226]{0,1:T(8,128)S(1)} %pad_convert_fusion), kind=kLoop, calls=%fused_computation.281 | loop fusion | bytes 63922176 | tf_op jit(solution)/shard_map/jvp()/slice | solution.py:88
  234.0 4.6 copy.291
  256.1 4.6 copy.300
  290.0 24.3 %multiply_reduce_fusion.17 = (f32[6,1156]{0,1:T(8,128)}, f32[6,1156]{0,1:T(8,128)S(1)}, f32[6,1156]{0,1:T(8,128)S(1)}, f32[6,1156]{0,1:T(8,128)}, f32[6,1156]{0,...) fusion(f32[6,64,1156]{1,0,2:T(8,128)} %reshape.1855, ...), kind=kLoop, calls=%fused_computation.21 | loop fusion | flops 7927848 | bytes 18005856 | tf_op jit(solution)/shard_map/transpose(jvp())/reduce_sum | solution.py:55
  327.6 4.6 copy.262
  349.7 4.6 copy.271
  391.4 24.1 %multiply_reduce_fusion.16 = (f32[6,1156]{0,1:T(8,128)}, f32[6,1156]{0,1:T(8,128)S(1)}, f32[6,1156]{0,1:T(8,128)S(1)}, f32[6,1156]{0,1:T(8,128)}, f32[6,1156]{0,...) fusion(f32[6,64,1156]{1,0,2:T(8,128)} %reshape.1864, ...), kind=kLoop, calls=%fused_computation.20 | loop fusion | flops 7927848 | bytes 18005856 | tf_op jit(solution)/shard_map/jvp()/reduce_sum | solution.py:48
  461.3 4.7 bitcast_multiply_fusion.28
  466.1 5.6 bitcast_multiply_fusion.29
  493.1 9.4 pad_add_fusion.13
  502.5 10.4 %pad_add_fusion.1 = f32[768,1156]{1,0:T(8,128)} fusion(f32[768,1156]{1,0:T(8,128)} %pad_add_fusion.7, f32[768,1156]{1,0:T(8,128)S(1)} %pad_add_fusion.8, f32[768,1156]{1,0:T(8,128)S(1)} %pad_add_fusion.9, f32[768,1156]{1,0:T(8,128)S(1)} %pad_add_fusion.10, f32[768,1156]{1,0:T(8,128)S(1)} %pad_add_fusion.11, f32[768,1156]{1,0:T(8,128)S(1)} %pad_add_fusion.12, ...), kind=kLoop, calls=%fused_computation.22 | loop fusion | flops 5326848 | bytes 28409856 | tf_op jit(solution)/shard_map/transpose(jvp())/add_any | solution.py:87
  512.9 5.3 copy.367
  518.2 4.7 reshape.1894
  531.9 5.1 broadcast_in_dim.184
  541.2 5.2 broadcast_in_dim.186
  550.4 5.2 broadcast_in_dim.182
  559.7 5.2 broadcast_in_dim.188
  568.9 5.2 broadcast_in_dim.190
  578.2 5.1 broadcast_in_dim.192
  587.4 5.2 broadcast_in_dim.194
  596.7 5.0 broadcast_in_dim.196
  606.2 5.2 broadcast_in_dim.198
  622.0 4.7 fusion.28
  642.5 9.2 bitcast_multiply_fusion.10
  651.8 12.2 %fusion.89 = (bf16[6,768,1024]{2,1,0:T(8,128)(2,1)S(1)}, f32[6,768,1024]{2,1,0:T(8,128)}) fusion(f32[1,384,1024]{2,1,0:T(8,128)} %bitcast.394, f32[1,384,1024]{2,1,0:T(8,128)} %bitcast.395, f32[1,384,1024]{2,1,0:T(8,128)} %bitcast.396, f32[1,384,1024]{2,1,0:T(8,128)} %bitcast.397, f32[1,384,1024]{2,1,0:T(8,128)} %bitcast.398, ...), kind=kLoop, calls=%fused_computation.278 | loop fusion | flops 56623104 | bytes 47185920 | tf_op jit(solution)/shard_map/convert.12
  667.5 4.7 collective-permute-start.9
  704.2 4.6 mul.1908
  708.8 5.1 mul.2017
  718.1 5.1 mul.2011
  727.3 5.2 mul.2013
  736.5 5.1 mul.2015
  745.8 5.1 mul.2019
  755.0 5.1 mul.2021
  764.3 5.2 mul.2023
  773.5 5.1 mul.2025
  782.8 5.6 mul.2027
  796.0 4.8 multiply_add_fusion
  800.9 9.7 %convolution_bitcast_fusion.1 = f32[1,384,384]{2,1,0:T(8,128)S(1)} fusion(f32[32,32,384]{2,1,0:T(8,128)S(1)} %copy-done.15, f32[384,34,34]{0,2,1:T(8,128)} %reshape.1907, f32[384,34,34]{0,2,1:T(8,128)} %mul.2027, f32[384,34,34]{0,2,1:T(8,128)} %reshape.1906, f32[384,34,34]{0,2,1:T(8,128)} %mul.2025, f32[384,34,34]{0,2,1:T(8,128)} %reshape.1905, ...), kind=kOutput, calls=%fused_computation.162 | convolution fusion | flops 1815871488 | bytes 17891328 | tf_op jit(solution)/shard_map/dn,ne->de/dot_general | solution.py:226
  812.1 6.3 fusion
  833.2 7.4 fusion.5
  846.7 30.4 %psum.23 = f32[2,384]{1,0:T(2,128)S(1)} all-reduce(f32[2,384]{1,0:T(2,128)S(1)} %pad_maximum_fusion.4), channel_id=1, replica_groups=mesh['group'=2,'lon'=8,'lat'=2] {'lon','lat'}, use_global_device_ids=true, to_apply=%region_42.43 | all-reduce | flops 768 | bytes 6144 | tf_op jit(solution)/shard_map/psum | solution.py:278
  880.6 66.4 %all-reduce.49.cloned.1.call-done = (f32[2,384,1152]{2,1,0:T(8,128)}, f32[2,384,384]{2,1,0:T(8,128)}) async-done(((f32[2,384,1152]{2,1,0:T(8,128)}, f32[2,384,384]{2,1,0:T(8,128)}), (f32[2,384,1152]{2,1,0:T(8,128)}, f32[2,384,384]{2,1,0:T(8,128)})) %all-reduce.49.cloned.1.call-update) | async-done | bytes 4718608 | tf_op jit(solution)/shard_map/psum | solution.py:278
  (579 shorter events, 425.8 us)
Async XLA Ops:
  7.2 939.8 %all-reduce.49.cloned.1.call-start = ((), (), s32[]{:S(2)}) async-start(), calls=%async_computation | async-start | bytes 9437184 | tf_op jit(solution)/shard_map/psum | solution.py:278
  7.9 7.8 copy-start.164
  13.3 178.8 %copy-start.176 = (f32[384]{0:T(512)}, f32[384]{0:T(512)S(1)}, u32[]{:S(2)}) copy-start(f32[384]{0:T(512)S(1)} %get-tuple-element.38) | copy-start | bytes 4612
  17.2 22.9 %copy-start.36 = (bf16[32,32,384]{2,1,0:T(8,128)(2,1)}, bf16[32,32,384]{2,1,0:T(8,128)(2,1)S(1)}, u32[]{:S(2)}) copy-start(bf16[32,32,384]{2,1,0:T(8,128)(2,1)S(1)} %get-tuple-element.114) | copy-start | bytes 2359300
  18.3 3.5 collective-permute-start
  21.8 8.8 copy-start.13
  21.8 8.8 copy-start.102
  24.2 138.3 %collective-permute-start.1 = (bf16[2,768,1024]{2,1,0:T(8,128)(2,1)}, bf16[2,768,1024]{2,1,0:T(8,128)(2,1)}, u32[]{:S(2)}, u32[]{:S(2)}) collective-permute-start(bf16[2,768,1024]{2,1,0:T(8,128)(2,1)} %pad_maximum_fusion.1), channel_id=1, source_target_pairs={{0,2},{2,4},{4,6},{6,8},{8,10},{10,12},{12,14},{14,0},{1,3},{3,5},... | collective-permute-start | bytes 9437192 | tf_op jit(solution)/shard_map/ppermute | solution.py:18
  27.1 138.1 %collective-permute-start.2 = (bf16[2,768,1024]{2,1,0:T(8,128)(2,1)}, bf16[2,768,1024]{2,1,0:T(8,128)(2,1)}, u32[]{:S(2)}, u32[]{:S(2)}) collective-permute-start(bf16[2,768,1024]{2,1,0:T(8,128)(2,1)} %pad_maximum_fusion.1), channel_id=1, source_target_pairs={{0,14},{2,0},{4,2},{6,4},{8,6},{10,8},{12,10},{14,12},{1,15},{3,1}... | collective-permute-start | bytes 9437192 | tf_op jit(solution)/shard_map/ppermute | solution.py:18
  170.0 12.1 %copy-start = (f32[6,768,1024]{2,1,0:T(8,128)}, f32[6,768,1024]{2,1,0:T(8,128)S(1)}, u32[]{:S(2)}) copy-start(f32[6,768,1024]{2,1,0:T(8,128)S(1)} %maximum_convert_fusion) | copy-start | bytes 56623108
  193.7 1.3 collective-permute-start.3
  195.4 12.1 %collective-permute-start.4 = (bf16[768,34,1]{0,2,1:T(2,128)(2,1)S(1)}, bf16[768,34,1]{0,2,1:T(2,128)(2,1)S(1)}, u32[]{:S(2)}, u32[]{:S(2)}) collective-permute-start(bf16[768,34,1]{0,2,1:T(2,128)(2,1)S(1)} %get-tuple-element.106), channel_id=1, source_target_pairs={{0,2},{2,4},{4,6},{6,8},{8,10},{10,12},{12,14},{14,0},{1,3},{3,5},... | collective-permute-start | bytes 156680 | tf_op jit(solution)/shard_map/ppermute | solution.py:28
  195.5 12.1 %collective-permute-start.5 = (bf16[768,34,1]{0,2,1:T(2,128)(2,1)S(1)}, bf16[768,34,1]{0,2,1:T(2,128)(2,1)S(1)}, u32[]{:S(2)}, u32[]{:S(2)}) collective-permute-start(bf16[768,34,1]{0,2,1:T(2,128)(2,1)S(1)} %get-tuple-element.107), channel_id=1, source_target_pairs={{2,0},{4,2},{6,4},{8,6},{10,8},{12,10},{14,12},{0,14},{3,1},{5,3},... | collective-permute-start | bytes 156680 | tf_op jit(solution)/shard_map/ppermute | solution.py:30
  317.4 109.0 %copy-start.131 = (f32[6,1156]{1,0:T(8,128)}, f32[6,1156]{1,0:T(8,128)S(1)}, u32[]{:S(2)}) copy-start(f32[6,1156]{1,0:T(8,128)S(1)} %copy.292) | copy-start | bytes 83236
  318.8 107.7 %copy-start.132 = (f32[6,1156]{1,0:T(8,128)}, f32[6,1156]{1,0:T(8,128)S(1)}, u32[]{:S(2)}) copy-start(f32[6,1156]{1,0:T(8,128)S(1)} %copy.295) | copy-start | bytes 83236
  325.2 101.3 %copy-start.133 = (f32[6,1156]{1,0:T(8,128)}, f32[6,1156]{1,0:T(8,128)S(1)}, u32[]{:S(2)}) copy-start(f32[6,1156]{1,0:T(8,128)S(1)} %copy.307) | copy-start | bytes 83236
  325.4 101.0 %copy-start.134 = (f32[6,1156]{1,0:T(8,128)}, f32[6,1156]{1,0:T(8,128)S(1)}, u32[]{:S(2)}) copy-start(f32[6,1156]{1,0:T(8,128)S(1)} %copy.310) | copy-start | bytes 83236
  325.7 100.8 %copy-start.135 = (f32[6,1156]{1,0:T(8,128)}, f32[6,1156]{1,0:T(8,128)S(1)}, u32[]{:S(2)}) copy-start(f32[6,1156]{1,0:T(8,128)S(1)} %copy.313) | copy-start | bytes 83236
  427.5 38.5 %copy-start.125 = (f32[6,1156]{1,0:T(8,128)}, f32[6,1156]{1,0:T(8,128)S(1)}, u32[]{:S(2)}) copy-start(f32[6,1156]{1,0:T(8,128)S(1)} %get-tuple-element.130) | copy-start | bytes 83236
  429.1 36.9 %copy-start.126 = (f32[6,1156]{1,0:T(8,128)}, f32[6,1156]{1,0:T(8,128)S(1)}, u32[]{:S(2)}) copy-start(f32[6,1156]{1,0:T(8,128)S(1)} %get-tuple-element.133) | copy-start | bytes 83236
  429.1 36.9 %copy-start.127 = (f32[6,1156]{1,0:T(8,128)}, f32[6,1156]{1,0:T(8,128)S(1)}, u32[]{:S(2)}) copy-start(f32[6,1156]{1,0:T(8,128)S(1)} %get-tuple-element.138) | copy-start | bytes 83236
  525.5 101.2 %collective-permute-start.6 = (bf16[768,34,1]{0,2,1:T(2,128)(2,1)S(1)}, bf16[768,34,1]{0,2,1:T(2,128)(2,1)S(1)}, u32[]{:S(2)}, u32[]{:S(2)}) collective-permute-start(bf16[768,34,1]{0,2,1:T(2,128)(2,1)S(1)} %get-tuple-element.84), channel_id=1, source_target_pairs={{0,14},{2,0},{4,2},{6,4},{8,6},{10,8},{12,10},{14,12},{1,15},{3,1}... | collective-permute-start | bytes 156680 | tf_op jit(solution)/shard_map/ppermute | solution.py:18
  525.8 101.0 %collective-permute-start.7 = (bf16[768,34,1]{0,2,1:T(2,128)(2,1)S(1)}, bf16[768,34,1]{0,2,1:T(2,128)(2,1)S(1)}, u32[]{:S(2)}, u32[]{:S(2)}) collective-permute-start(bf16[768,34,1]{0,2,1:T(2,128)(2,1)S(1)} %get-tuple-element.85), channel_id=1, source_target_pairs={{0,2},{2,4},{4,6},{6,8},{8,10},{10,12},{12,14},{14,0},{1,3},{3,5},... | collective-permute-start | bytes 156680 | tf_op jit(solution)/shard_map/ppermute | solution.py:18
  627.4 2.7 collective-permute-start.8
  636.3 182.4 %copy-start.7 = (f32[32,32,384]{2,1,0:T(8,128)}, f32[32,32,384]{2,1,0:T(8,128)S(1)}, u32[]{:S(2)}) copy-start(f32[32,32,384]{2,1,0:T(8,128)S(1)} %add_add_fusion.2) | copy-start | bytes 4718596
  642.4 9.3 copy-start.158
  642.5 9.2 copy-start.138
  642.5 9.2 copy-start.140
  642.5 9.2 copy-start.142
  642.5 9.2 copy-start.144
  667.4 12.2 %copy-start.12 = (f32[384,1156]{0,1:T(8,128)S(1)}, f32[384,1156]{0,1:T(8,128)}, u32[]{:S(2)}) copy-start(f32[384,1156]{0,1:T(8,128)} %get-tuple-element.67) | copy-start | bytes 5326852
  667.4 144.6 %collective-permute-start.10 = (bf16[2,768,1024]{2,1,0:T(8,128)(2,1)}, bf16[2,768,1024]{2,1,0:T(8,128)(2,1)}, u32[]{:S(2)}, u32[]{:S(2)}) collective-permute-start(bf16[2,768,1024]{2,1,0:T(8,128)(2,1)} %get-tuple-element.65), channel_id=1, source_target_pairs={{0,2},{2,4},{4,6},{6,8},{8,10},{10,12},{12,14},{14,0},{1,3},{3,5},... | collective-permute-start | bytes 9437192 | tf_op jit(solution)/shard_map/ppermute | solution.py:18
  667.5 144.6 %collective-permute-start.9 = (bf16[2,768,1024]{2,1,0:T(8,128)(2,1)}, bf16[2,768,1024]{2,1,0:T(8,128)(2,1)}, u32[]{:S(2)}, u32[]{:S(2)}) collective-permute-start(bf16[2,768,1024]{2,1,0:T(8,128)(2,1)} %get-tuple-element.64), channel_id=1, source_target_pairs={{0,14},{2,0},{4,2},{6,4},{8,6},{10,8},{12,10},{14,12},{1,15},{3,1}... | collective-permute-start | bytes 9437192 | tf_op jit(solution)/shard_map/ppermute | solution.py:18
  782.8 9.5 copy-start.84
  800.8 9.8 %copy-start.28 = (f32[1,384,1024]{2,1,0:T(8,128)S(1)}, f32[1,384,1024]{2,1,0:T(8,128)}, u32[]{:S(2)}) copy-start(f32[1,384,1024]{2,1,0:T(8,128)} %get-tuple-element.52) | copy-start | bytes 4718596
  800.8 9.8 %copy-start.29 = (f32[1,384,1024]{2,1,0:T(8,128)S(1)}, f32[1,384,1024]{2,1,0:T(8,128)}, u32[]{:S(2)}) copy-start(f32[1,384,1024]{2,1,0:T(8,128)} %get-tuple-element.59) | copy-start | bytes 4718596
  800.8 9.9 %copy-start.30 = (f32[1,384,1024]{2,1,0:T(8,128)S(1)}, f32[1,384,1024]{2,1,0:T(8,128)}, u32[]{:S(2)}) copy-start(f32[1,384,1024]{2,1,0:T(8,128)} %get-tuple-element.60) | copy-start | bytes 4718596
  800.9 9.9 %copy-start.31 = (f32[1,384,1024]{2,1,0:T(8,128)S(1)}, f32[1,384,1024]{2,1,0:T(8,128)}, u32[]{:S(2)}) copy-start(f32[1,384,1024]{2,1,0:T(8,128)} %get-tuple-element.61) | copy-start | bytes 4718596
  800.9 9.9 %copy-start.32 = (f32[1,384,1024]{2,1,0:T(8,128)S(1)}, f32[1,384,1024]{2,1,0:T(8,128)}, u32[]{:S(2)}) copy-start(f32[1,384,1024]{2,1,0:T(8,128)} %get-tuple-element.62) | copy-start | bytes 4718596
  800.9 9.9 %copy-start.33 = (f32[1,384,1024]{2,1,0:T(8,128)S(1)}, f32[1,384,1024]{2,1,0:T(8,128)}, u32[]{:S(2)}) copy-start(f32[1,384,1024]{2,1,0:T(8,128)} %get-tuple-element.63) | copy-start | bytes 4718596
  800.9 9.9 %copy-start.139 = (f32[6,1024]{1,0:T(8,128)S(1)}, f32[6,1024]{1,0:T(8,128)}, u32[]{:S(2)}) copy-start(f32[6,1024]{1,0:T(8,128)} %copy-done.138) | copy-start | bytes 73732
  800.9 9.9 %copy-start.141 = (f32[6,1024]{1,0:T(8,128)S(1)}, f32[6,1024]{1,0:T(8,128)}, u32[]{:S(2)}) copy-start(f32[6,1024]{1,0:T(8,128)} %copy-done.140) | copy-start | bytes 73732
  800.9 9.9 %copy-start.143 = (f32[6,1024]{1,0:T(8,128)S(1)}, f32[6,1024]{1,0:T(8,128)}, u32[]{:S(2)}) copy-start(f32[6,1024]{1,0:T(8,128)} %copy-done.142) | copy-start | bytes 73732
  800.9 9.9 %copy-start.145 = (f32[6,1024]{1,0:T(8,128)S(1)}, f32[6,1024]{1,0:T(8,128)}, u32[]{:S(2)}) copy-start(f32[6,1024]{1,0:T(8,128)} %copy-done.144) | copy-start | bytes 73732
  800.9 9.9 %copy-start.159 = (f32[6,1024]{1,0:T(8,128)S(1)}, f32[6,1024]{1,0:T(8,128)}, u32[]{:S(2)}) copy-start(f32[6,1024]{1,0:T(8,128)} %copy-done.158) | copy-start | bytes 73732
  818.4 8.7 copy-start.4
  818.7 8.4 collective-permute-start.11
  833.2 7.4 copy-start.78
  (143 other events, 453.8 us)
Sparse Core Ops, SparseCore 0:
  832.2 114.7 all-reduce.48
where the time goes:
time: 967 us; the launch traced here: 959 us
  local copies, waits for them, and re-layouts  465 us (48%)
  waiting for transfers between devices  192 us (20%)
  other arithmetic  190 us (20%)
  matrix products  46.3 us (5%)
  blocking collectives  30.4 us (3%)
  starting transfers between devices  18.9 us (2%)
  between operations  16.3 us (2%)
    ppermute x6, waiting for transfers between devices, passed_along(): return lax.ppermute(value, axis, pairs)  122 us
    mul x18, local copies, waits for them, and re-layouts, mix_heads(): result = result + (weight_one / weight_sum)[:, None, :] * value_one  84.1 us
    broadcast_in_dim x18, local copies, waits for them, and re-layouts, mix_heads(): jnp.sum(query_heads * key_one, axis=1) * head_size ** (-0.5)  83.7 us
    psum x1, waiting for transfers between devices, local(): lax.psum((jnp.stack([qkv_first, qkv_second]), jnp.stack([out_first, out_s...  66.4 us
    reshape x18, local copies, waits for them, and re-layouts, plain_mix(): key_list.append(window[:width].reshape(HEADS, head_size, points))  63.9 us
    reshape x18, local copies, waits for them, and re-layouts, plain_mix(): value_list.append(window[width:].reshape(HEADS, head_size, points))  59.8 us
    unnamed x365, local copies, waits for them, and re-layouts  39.3 us
    slice x10, local copies, waits for them, and re-layouts, plain_mix(): key_list.append(window[:width].reshape(HEADS, head_size, points))  35.1 us
  transfers between devices with their start and end apart: 13, of which 5 were waited for; matrix products, arithmetic and copies ran while one was open for 29% of the time, Pallas kernels for 0%

commit v1 on v0

--- a/solution.py
+++ b/solution.py
@@ -4,6 +4,11 @@
 from jax.sharding import PartitionSpec as P
 
 HEADS = 6
+
+
+def axis_by_axis(array, first, second):
+    partial = lax.psum(array, first)
+    return lax.psum(partial, second)
 
 
 def partner(value, axis, stride):
@@ -275,13 +280,14 @@
         gradient_between, saved_first, query_key_value_weight[0], output_weight[0]
     )
     grad_tokens = jnp.where(shown, grad_start.reshape(row_count, col_count, width), 0.0)
-    summed_qkv, summed_out, summed_gain = lax.psum(
+    summed_qkv, summed_out, summed_gain = axis_by_axis(
         (
             jnp.stack([qkv_first, qkv_second]),
             jnp.stack([out_first, out_second]),
             jnp.stack([gain_first, gain_second]),
         ),
-        ("lon", "lat"),
+        "lat",
+        "lon",
     )
     factor = (row_count * col_count * lat_count * lon_count) ** (-0.5)
     return (grad_tokens, summed_qkv * factor, summed_out * factor, summed_gain * factor)

time: 967 us -> 1050 us (1.086)
  waiting for transfers between devices: 192 us -> 285 us
    psum x1 -> x2, waiting for transfers between devices: 66.4 us -> 160 us  [the longest x1 133 us: axis_by_axis(): return lax.psum(partial, second)]
    psum x1 -> x2, blocking collectives: 30.4 us -> 25 us  [the longest x1 22.5 us: axis_by_axis(): return lax.psum(partial, second)]
  transfers between devices with their start and end apart: 13 -> 14, of which waited for: 5 -> 6; matrix products, arithmetic and copies ran while one was open for 29% -> 26% of each run, Pallas kernels for 0% -> 0%
where the time goes in v1:
time: 1050 us
  local copies, waits for them, and re-layouts  465 us (44%)
  waiting for transfers between devices  285 us (27%)
  other arithmetic  190 us (18%)
  matrix products  45.7 us (4%)
  blocking collectives  25 us (2%)
  starting transfers between devices  18.9 us (2%)
  between operations  16.3 us (2%)
    psum x1, waiting for transfers between devices, axis_by_axis(): return lax.psum(partial, second)  133 us
    ppermute x6, waiting for transfers between devices, passed_along(): return lax.ppermute(value, axis, pairs)  122 us
    mul x18, local copies, waits for them, and re-layouts, mix_heads(): result = result + (weight_one / weight_sum)[:, None, :] * value_one  84.2 us
    broadcast_in_dim x18, local copies, waits for them, and re-layouts, mix_heads(): jnp.sum(query_heads * key_one, axis=1) * head_size ** (-0.5)  83.8 us
    reshape x18, local copies, waits for them, and re-layouts, plain_mix(): key_list.append(window[:width].reshape(HEADS, head_size, points))  64 us
    reshape x18, local copies, waits for them, and re-layouts, plain_mix(): value_list.append(window[width:].reshape(HEADS, head_size, points))  59.8 us
    unnamed x365, local copies, waits for them, and re-layouts  39.3 us
    slice x10, local copies, waits for them, and re-layouts, plain_mix(): key_list.append(window[:width].reshape(HEADS, head_size, points))  35.3 us
  transfers between devices with their start and end apart: 14, of which 6 were waited for; matrix products, arithmetic and copies ran while one was open for 26% of the time, Pallas kernels for 0%

profile of v1, /device:TPU:0, one launch (start us, length us, event | category | flops | bytes accessed | tf_op | source)
XLA Modules:
  0.0 1046.6 jit_solution(14243752203043007502)
XLA Ops:
  43.2 119.3 %collective-permute-done.1 = bf16[2,768,1024]{2,1,0:T(8,128)(2,1)} collective-permute-done((bf16[2,768,1024]{2,1,0:T(8,128)(2,1)}, bf16[2,768,1024]{2,1,0:T(8,128)(2,1)}, u32[]{:S(2)}, u32[]{:S(2)}) %collective-permute-start.1) | collective-permute-done | bytes 3145760 | tf_op jit(solution)/shard_map/ppermute | solution.py:23
  165.1 4.8 maximum_convert_fusion
  169.9 6.6 fusion.90
  176.6 5.4 copy-done
  182.0 6.0 multiply_reduce_fusion.26
  195.4 4.9 collective-permute-start.5
  213.7 10.3 fusion.92
  234.1 4.6 copy.291
  290.1 24.3 %multiply_reduce_fusion.17 = (f32[6,1156]{0,1:T(8,128)}, f32[6,1156]{0,1:T(8,128)S(1)}, f32[6,1156]{0,1:T(8,128)S(1)}, f32[6,1156]{0,1:T(8,128)}, f32[6,1156]{0,...) fusion(f32[6,64,1156]{1,0,2:T(8,128)} %reshape.1855, ...), kind=kLoop, calls=%fused_computation.21 | loop fusion | flops 7927848 | bytes 18005856 | tf_op jit(solution)/shard_map/transpose(jvp())/reduce_sum | solution.py:60
  327.7 4.6 copy.262
  349.9 4.6 copy.271
  391.5 24.1 %multiply_reduce_fusion.16 = (f32[6,1156]{0,1:T(8,128)}, f32[6,1156]{0,1:T(8,128)S(1)}, f32[6,1156]{0,1:T(8,128)S(1)}, f32[6,1156]{0,1:T(8,128)}, f32[6,1156]{0,...) fusion(f32[6,64,1156]{1,0,2:T(8,128)} %reshape.1864, ...), kind=kLoop, calls=%fused_computation.20 | loop fusion | flops 7927848 | bytes 18005856 | tf_op jit(solution)/shard_map/jvp()/reduce_sum | solution.py:53
  461.5 4.7 bitcast_multiply_fusion.28
  466.2 5.6 bitcast_multiply_fusion.29
  493.2 9.4 pad_add_fusion.13
  502.6 10.4 pad_add_fusion.1
  513.0 5.3 copy.367
  518.4 4.7 reshape.1894
  532.1 5.1 broadcast_in_dim.184
  541.3 5.1 broadcast_in_dim.186
  550.6 5.1 broadcast_in_dim.182
  559.9 5.1 broadcast_in_dim.188
  569.1 5.2 broadcast_in_dim.190
  578.4 5.1 broadcast_in_dim.192
  587.6 5.1 broadcast_in_dim.194
  596.8 5.0 broadcast_in_dim.196
  606.4 5.2 broadcast_in_dim.198
  622.2 4.7 fusion.28
  642.7 9.2 bitcast_multiply_fusion.10
  651.9 12.2 %fusion.89 = (bf16[6,768,1024]{2,1,0:T(8,128)(2,1)S(1)}, f32[6,768,1024]{2,1,0:T(8,128)}) fusion(f32[1,384,1024]{2,1,0:T(8,128)} %bitcast.394, f32[1,384,1024]{2,1,0:T(8,128)} %bitcast.395, f32[1,384,1024]{2,1,0:T(8,128)} %bitcast.396, f32[1,384,1024]{2,1,0:T(8,128)} %bitcast.397, f32[1,384,1024]{2,1,0:T(8,128)} %bitcast.398, ...), kind=kLoop, calls=%fused_computation.278 | loop fusion | flops 56623104 | bytes 47185920 | tf_op jit(solution)/shard_map/convert.12
  667.6 4.7 collective-permute-start.9
  704.4 4.6 mul.1908
  709.0 5.1 mul.2017
  718.2 5.1 mul.2011
  727.5 5.1 mul.2013
  736.7 5.2 mul.2015
  746.0 5.1 mul.2019
  755.2 5.1 mul.2021
  764.5 5.2 mul.2023
  773.8 5.1 mul.2025
  783.0 5.6 mul.2027
  796.3 4.8 multiply_add_fusion
  801.2 9.7 convolution_bitcast_fusion.1
  812.3 6.3 fusion
  832.3 26.6 %all-reduce.53.cloned.1.call-done = (f32[2,384,1152]{2,1,0:T(8,128)}, f32[2,384,384]{2,1,0:T(8,128)}) async-done(((f32[2,384,1152]{2,1,0:T(8,128)}, f32[2,384,384]{2,1,0:T(8,128)}), (f32[2,384,1152]{2,1,0:T(8,128)}, f32[2,384,384]{2,1,0:T(8,128)})) %all-reduce.53.cloned.1.call-update) | async-done | bytes 4718608 | tf_op jit(solution)/shard_map/psum | solution.py:10
  860.1 7.1 fusion.5
  875.4 22.5 %psum.47 = f32[2,384]{1,0:T(2,128)S(1)} all-reduce(f32[2,384]{1,0:T(2,128)S(1)} %psum.46), channel_id=1, replica_groups=mesh['group'=2,'lon'=8,'lat'=2] {'lon'}, use_global_device_ids=true, to_apply=%region_45.46 | all-reduce | flops 768 | bytes 6144 | tf_op jit(solution)/shard_map/psum | solution.py:11
  901.4 133.0 %all-reduce.51.cloned.1.call-done = (f32[2,384,1152]{2,1,0:T(8,128)}, f32[2,384,384]{2,1,0:T(8,128)}) async-done(((f32[2,384,1152]{2,1,0:T(8,128)}, f32[2,384,384]{2,1,0:T(8,128)}), (f32[2,384,1152]{2,1,0:T(8,128)}, f32[2,384,384]{2,1,0:T(8,128)})) %all-reduce.51.cloned.1.call-update) | async-done | bytes 4718608 | tf_op jit(solution)/shard_map/psum | solution.py:11
  (583 shorter events, 432.6 us)
Async XLA Ops:
  7.2 851.7 %all-reduce.53.cloned.1.call-start = ((), (), s32[]{:S(2)}) async-start(), calls=%async_computation.1 | async-start | bytes 9437184 | tf_op jit(solution)/shard_map/psum | solution.py:10
  7.9 7.8 copy-start.164
  13.3 178.7 %copy-start.176 = (f32[384]{0:T(512)}, f32[384]{0:T(512)S(1)}, u32[]{:S(2)}) copy-start(f32[384]{0:T(512)S(1)} %get-tuple-element.38) | copy-start | bytes 4612
  17.2 22.9 %copy-start.36 = (bf16[32,32,384]{2,1,0:T(8,128)(2,1)}, bf16[32,32,384]{2,1,0:T(8,128)(2,1)S(1)}, u32[]{:S(2)}) copy-start(bf16[32,32,384]{2,1,0:T(8,128)(2,1)S(1)} %get-tuple-element.116) | copy-start | bytes 2359300
  18.3 3.6 collective-permute-start
  21.8 8.7 copy-start.13
  21.8 8.7 copy-start.102
  24.2 138.3 %collective-permute-start.1 = (bf16[2,768,1024]{2,1,0:T(8,128)(2,1)}, bf16[2,768,1024]{2,1,0:T(8,128)(2,1)}, u32[]{:S(2)}, u32[]{:S(2)}) collective-permute-start(bf16[2,768,1024]{2,1,0:T(8,128)(2,1)} %pad_maximum_fusion.1), channel_id=1, source_target_pairs={{0,2},{2,4},{4,6},{6,8},{8,10},{10,12},{12,14},{14,0},{1,3},{3,5},... | collective-permute-start | bytes 9437192 | tf_op jit(solution)/shard_map/ppermute | solution.py:23
  27.1 138.0 %collective-permute-start.2 = (bf16[2,768,1024]{2,1,0:T(8,128)(2,1)}, bf16[2,768,1024]{2,1,0:T(8,128)(2,1)}, u32[]{:S(2)}, u32[]{:S(2)}) collective-permute-start(bf16[2,768,1024]{2,1,0:T(8,128)(2,1)} %pad_maximum_fusion.1), channel_id=1, source_target_pairs={{0,14},{2,0},{4,2},{6,4},{8,6},{10,8},{12,10},{14,12},{1,15},{3,1}... | collective-permute-start | bytes 9437192 | tf_op jit(solution)/shard_map/ppermute | solution.py:23
  169.9 12.1 %copy-start = (f32[6,768,1024]{2,1,0:T(8,128)}, f32[6,768,1024]{2,1,0:T(8,128)S(1)}, u32[]{:S(2)}) copy-start(f32[6,768,1024]{2,1,0:T(8,128)S(1)} %maximum_convert_fusion) | copy-start | bytes 56623108
  193.6 1.3 collective-permute-start.3
  195.4 12.1 %collective-permute-start.4 = (bf16[768,34,1]{0,2,1:T(2,128)(2,1)S(1)}, bf16[768,34,1]{0,2,1:T(2,128)(2,1)S(1)}, u32[]{:S(2)}, u32[]{:S(2)}) collective-permute-start(bf16[768,34,1]{0,2,1:T(2,128)(2,1)S(1)} %get-tuple-element.108), channel_id=1, source_target_pairs={{0,2},{2,4},{4,6},{6,8},{8,10},{10,12},{12,14},{14,0},{1,3},{3,5},... | collective-permute-start | bytes 156680 | tf_op jit(solution)/shard_map/ppermute | solution.py:33
  195.4 12.0 %collective-permute-start.5 = (bf16[768,34,1]{0,2,1:T(2,128)(2,1)S(1)}, bf16[768,34,1]{0,2,1:T(2,128)(2,1)S(1)}, u32[]{:S(2)}, u32[]{:S(2)}) collective-permute-start(bf16[768,34,1]{0,2,1:T(2,128)(2,1)S(1)} %get-tuple-element.109), channel_id=1, source_target_pairs={{2,0},{4,2},{6,4},{8,6},{10,8},{12,10},{14,12},{0,14},{3,1},{5,3},... | collective-permute-start | bytes 156680 | tf_op jit(solution)/shard_map/ppermute | solution.py:35
  317.6 109.0 %copy-start.131 = (f32[6,1156]{1,0:T(8,128)}, f32[6,1156]{1,0:T(8,128)S(1)}, u32[]{:S(2)}) copy-start(f32[6,1156]{1,0:T(8,128)S(1)} %copy.292) | copy-start | bytes 83236
  318.9 107.7 %copy-start.132 = (f32[6,1156]{1,0:T(8,128)}, f32[6,1156]{1,0:T(8,128)S(1)}, u32[]{:S(2)}) copy-start(f32[6,1156]{1,0:T(8,128)S(1)} %copy.295) | copy-start | bytes 83236
  325.3 101.3 %copy-start.133 = (f32[6,1156]{1,0:T(8,128)}, f32[6,1156]{1,0:T(8,128)S(1)}, u32[]{:S(2)}) copy-start(f32[6,1156]{1,0:T(8,128)S(1)} %copy.307) | copy-start | bytes 83236
  325.5 101.0 %copy-start.134 = (f32[6,1156]{1,0:T(8,128)}, f32[6,1156]{1,0:T(8,128)S(1)}, u32[]{:S(2)}) copy-start(f32[6,1156]{1,0:T(8,128)S(1)} %copy.310) | copy-start | bytes 83236
  325.8 100.8 %copy-start.135 = (f32[6,1156]{1,0:T(8,128)}, f32[6,1156]{1,0:T(8,128)S(1)}, u32[]{:S(2)}) copy-start(f32[6,1156]{1,0:T(8,128)S(1)} %copy.313) | copy-start | bytes 83236
  427.7 38.5 %copy-start.125 = (f32[6,1156]{1,0:T(8,128)}, f32[6,1156]{1,0:T(8,128)S(1)}, u32[]{:S(2)}) copy-start(f32[6,1156]{1,0:T(8,128)S(1)} %get-tuple-element.132) | copy-start | bytes 83236
  429.2 36.9 %copy-start.126 = (f32[6,1156]{1,0:T(8,128)}, f32[6,1156]{1,0:T(8,128)S(1)}, u32[]{:S(2)}) copy-start(f32[6,1156]{1,0:T(8,128)S(1)} %get-tuple-element.135) | copy-start | bytes 83236
  429.2 36.9 %copy-start.127 = (f32[6,1156]{1,0:T(8,128)}, f32[6,1156]{1,0:T(8,128)S(1)}, u32[]{:S(2)}) copy-start(f32[6,1156]{1,0:T(8,128)S(1)} %get-tuple-element.140) | copy-start | bytes 83236
  525.7 101.2 %collective-permute-start.6 = (bf16[768,34,1]{0,2,1:T(2,128)(2,1)S(1)}, bf16[768,34,1]{0,2,1:T(2,128)(2,1)S(1)}, u32[]{:S(2)}, u32[]{:S(2)}) collective-permute-start(bf16[768,34,1]{0,2,1:T(2,128)(2,1)S(1)} %get-tuple-element.86), channel_id=1, source_target_pairs={{0,14},{2,0},{4,2},{6,4},{8,6},{10,8},{12,10},{14,12},{1,15},{3,1}... | collective-permute-start | bytes 156680 | tf_op jit(solution)/shard_map/ppermute | solution.py:23
  526.0 101.0 %collective-permute-start.7 = (bf16[768,34,1]{0,2,1:T(2,128)(2,1)S(1)}, bf16[768,34,1]{0,2,1:T(2,128)(2,1)S(1)}, u32[]{:S(2)}, u32[]{:S(2)}) collective-permute-start(bf16[768,34,1]{0,2,1:T(2,128)(2,1)S(1)} %get-tuple-element.87), channel_id=1, source_target_pairs={{0,2},{2,4},{4,6},{6,8},{8,10},{10,12},{12,14},{14,0},{1,3},{3,5},... | collective-permute-start | bytes 156680 | tf_op jit(solution)/shard_map/ppermute | solution.py:23
  627.6 2.7 collective-permute-start.8
  636.5 182.4 %copy-start.7 = (f32[32,32,384]{2,1,0:T(8,128)}, f32[32,32,384]{2,1,0:T(8,128)S(1)}, u32[]{:S(2)}) copy-start(f32[32,32,384]{2,1,0:T(8,128)S(1)} %add_add_fusion.2) | copy-start | bytes 4718596
  642.6 9.3 copy-start.158
  642.7 9.2 copy-start.138
  642.7 9.2 copy-start.140
  642.7 9.2 copy-start.142
  642.7 9.2 copy-start.144
  667.6 12.2 %copy-start.12 = (f32[384,1156]{0,1:T(8,128)S(1)}, f32[384,1156]{0,1:T(8,128)}, u32[]{:S(2)}) copy-start(f32[384,1156]{0,1:T(8,128)} %get-tuple-element.69) | copy-start | bytes 5326852
  667.6 144.7 %collective-permute-start.10 = (bf16[2,768,1024]{2,1,0:T(8,128)(2,1)}, bf16[2,768,1024]{2,1,0:T(8,128)(2,1)}, u32[]{:S(2)}, u32[]{:S(2)}) collective-permute-start(bf16[2,768,1024]{2,1,0:T(8,128)(2,1)} %get-tuple-element.67), channel_id=1, source_target_pairs={{0,2},{2,4},{4,6},{6,8},{8,10},{10,12},{12,14},{14,0},{1,3},{3,5},... | collective-permute-start | bytes 9437192 | tf_op jit(solution)/shard_map/ppermute | solution.py:23
  667.6 144.7 %collective-permute-start.9 = (bf16[2,768,1024]{2,1,0:T(8,128)(2,1)}, bf16[2,768,1024]{2,1,0:T(8,128)(2,1)}, u32[]{:S(2)}, u32[]{:S(2)}) collective-permute-start(bf16[2,768,1024]{2,1,0:T(8,128)(2,1)} %get-tuple-element.66), channel_id=1, source_target_pairs={{0,14},{2,0},{4,2},{6,4},{8,6},{10,8},{12,10},{14,12},{1,15},{3,1}... | collective-permute-start | bytes 9437192 | tf_op jit(solution)/shard_map/ppermute | solution.py:23
  783.0 9.5 copy-start.84
  801.1 9.8 copy-start.28
  801.1 9.8 copy-start.29
  801.1 9.8 copy-start.30
  801.1 9.9 copy-start.31
  801.1 9.9 copy-start.32
  801.1 9.9 copy-start.33
  801.1 9.9 copy-start.139
  801.1 9.9 copy-start.141
  801.1 9.9 copy-start.143
  801.1 9.9 copy-start.145
  801.1 9.9 copy-start.159
  818.6 8.7 copy-start.4
  818.9 8.4 collective-permute-start.11
  832.3 202.1 %all-reduce.51.cloned.1.call-start = ((), (), s32[]{:S(2)}) async-start(), calls=%async_computation | async-start | bytes 9437184 | tf_op jit(solution)/shard_map/psum | solution.py:11
  (144 other events, 459.4 us)
Sparse Core Ops, SparseCore 0:
  832.4 26.4 all-reduce.52
  862.9 171.3 all-reduce.50
